TPU v7x, 512 devices: a whole 4x8x8 slice. The times are simulated.
512 devices in a mesh: dom: 32 (over y, x), plane: 16 (over z, core).
Axes of the slice: x: 4, y: 8, z: 8, core: 2. Of those that a mesh axis runs over, the one named last changes fastest.
Arguments:
- adjoint: float32 [3, 64, 9, 9, 1024], P(None, 'plane', None, None, 'dom'), may hold values from -6 to 6
- metric: float32 [4, 1024], P(None, 'dom'), may hold values from 0.5 to 2
- base_flow: float32 [2, 12, 5308416], P(None, None, ('dom', 'plane')), may hold values from -6 to 6
- edge_list: int32 [32, 5, 24], P('dom'), may hold values from -1 to 127, as said below
- flips: int32 [32, 5, 24], P('dom'), may hold values from 0 to 1, as said below
Outputs:
- adjoint_next: float32 [3, 64, 9, 9, 1024], P(None, 'plane', None, None, 'dom')
Inputs may be any that keep to these rules, and one draw needn't show every extreme that they name: `edge_list`: entries are -1 or a local edge id j * 32 + l; no edge appears twice in one partition; filled slots come first in each block; a slot is filled exactly where its pair (as the steps define it) is filled, so block 2 has an even count; some block of some partition has all 24 slots filled, and every partition has an empty slot. `flips`: paired slots carry the same flag.
All inputs are finite; a program needn't handle non-finite values.
Results may differ from a plain program's by a relative error of at most 0.0003.
Values sent between devices are 32-bit elements; how exact they have to be, the bound alone decides.
A program may use at most 64 MiB of HBM per device.

v0:
```python
import functools

import jax
import jax.numpy as jnp
import ml_dtypes
import numpy as np
from jax import lax
from jax.experimental import pallas as pl
from jax.experimental.pallas import tpu as pltpu
from jax.sharding import PartitionSpec as P

MODES = 64
STEPS = 2
NODES = 9
NPTS = NODES * NODES
ELEMS = 32
PLANE = 16
LOCAL = MODES // PLANE
SPAN_PTS = NPTS * ELEMS // PLANE
CAP = 24
REACH = 2
STEP_SIZE = 0.01
VISCOSITY = 0.02

ROWS = 88
KROWS = 96
WIRE = 56
BACK = 24
LEAD = 8
BASE_ROWS = 12 * NPTS * STEPS

F32 = jnp.float32
BF16 = jnp.bfloat16
MESH_ID = pl.DeviceIdType.MESH


def split_table(table):
    hi = table.astype(np.float32).astype(ml_dtypes.bfloat16)
    lo = (table - hi.astype(np.float64)).astype(np.float32).astype(ml_dtypes.bfloat16)
    return np.concatenate([hi, hi, lo], axis=1)


def derivative_tables():
    order = NODES - 1
    ids = np.arange(NODES)
    coords = -np.cos(np.pi * ids / order)
    weight = np.where((ids == 0) | (ids == order), 2.0, 1.0)
    table = np.zeros((NODES, NODES))
    for a in range(NODES):
        for i in range(NODES):
            if a != i:
                table[a, i] = weight[a] / weight[i] * (-1.0) ** (a + i) / (coords[a] - coords[i])
    table -= np.diag(table.sum(axis=1))
    eye = np.eye(NODES)
    along_xi, along_eta = np.kron(table, eye), np.kron(eye, table)
    ops = [
        along_xi,
        along_eta,
        along_xi @ along_xi,
        along_xi @ along_eta,
        along_eta @ along_eta,
    ]
    stacked = np.zeros((len(ops) * ROWS, KROWS))
    for at, op in enumerate(ops):
        stacked[at * ROWS : at * ROWS + NPTS, :NPTS] = op
    return split_table(stacked)


def span_tables():
    modes = np.arange(MODES)
    wave = (modes + 1) // 2
    cosine = (modes % 2 == 1) | (modes == 0)
    angles = 2.0 * np.pi * ((np.arange(MODES)[:, None] * wave[None, :]) % MODES) / MODES
    basis = np.where(cosine[None, :], np.cos(angles), np.sin(angles))
    slope = np.where(cosine[None, :], -wave * np.sin(angles), wave * np.cos(angles))
    scale = np.where((modes == 0) | (modes == MODES - 1), 1.0 / MODES, 2.0 / MODES)
    forward = basis.T * scale[:, None]
    order = (np.arange(PLANE)[None, :] * LOCAL + np.arange(LOCAL)[:, None]).reshape(-1)
    span = np.concatenate([basis[:, order], slope[:, order]], axis=0)
    return split_table(span), split_table(forward[order])


def halves(x):
    hi = x.astype(BF16)
    return hi, (x - hi.astype(F32)).astype(BF16)


def three(x):
    hi, lo = halves(x)
    return jnp.concatenate([hi, lo, hi], axis=0)


def dot(a, b):
    return jnp.dot(a, b, preferred_element_type=F32)


def swap_blocks(parts):
    shape = parts[0].shape
    lane = lax.broadcasted_iota(jnp.int32, shape, 1)
    even = (lane // 32) % 2 == 0
    low = lane < 64
    a0, a1, a2, a3 = parts

    def near(x, y):
        return (
            jnp.where(even, x, pltpu.roll(y, 32, 1)),
            jnp.where(even, pltpu.roll(x, 96, 1), y),
        )

    def far(x, y):
        moved = pltpu.roll(jnp.where(low, y, x), 64, 1)
        return jnp.where(low, x, moved), jnp.where(low, moved, y)

    b0, b1 = near(a0, a1)
    b2, b3 = near(a2, a3)
    c0, c2 = far(b0, b2)
    c1, c3 = far(b1, b3)
    return [c0, c1, c2, c3]


def head(field):
    return [(field, k) for k in range(4)]


def tail(first, second):
    pair = [(first, 4), (first, 5)]
    return pair + ([(second, 4), (second, 5)] if second is not None else [None, None])


OUT_BLOCKS = (
    [head(0), head(1), head(2), tail(0, 1), tail(2, 3)]
    + [head(3), head(4), head(5), head(6), head(7), head(8)]
    + [tail(4, 5), tail(6, 7), tail(8, None)]
)
STATE_BLOCKS = 5
HEAD_AT = {0: 0, 1: 1, 2: 2, 3: 5, 4: 6, 5: 7, 6: 8, 7: 9, 8: 10}
TAIL_AT = {0: (3, 0), 1: (3, 1), 2: (4, 0), 3: (4, 1), 4: (11, 0), 5: (11, 1), 6: (12, 0), 7: (12, 1), 8: (13, 0)}


def kernel(
    n_dom,
    adj_ref,
    met_ref,
    base_ref,
    edge_ref,
    flip_ref,
    deriv_ref,
    span_ref,
    fwd_ref,
    out_ref,
    state,
    grads,
    base_in,
    base_head,
    base_tail,
    send_out,
    recv_out,
    send_back,
    recv_back,
    edge_out,
    edge_in,
    trace_a,
    trace_b,
    sums,
    send_hot,
    recv_hot,
    inv_weight,
    metrics,
    slot_ids,
    base_sem,
    out_send,
    out_recv,
    back_send,
    back_recv,
    edge_send,
    edge_recv,
):
    dom = lax.axis_index("dom")
    me = lax.axis_index("plane")

    barrier = pltpu.get_barrier_semaphore()

    def greet(distance, carry):
        pl.semaphore_signal(
            barrier, inc=1, device_id=(dom, lax.rem(me + distance, PLANE)), device_id_type=MESH_ID
        )
        return carry

    lax.fori_loop(1, PLANE, greet, 0)
    others = [block for block in range(2 * REACH + 1) if block != REACH]
    for block in others:
        pl.semaphore_signal(
            barrier,
            inc=1,
            device_id=(lax.rem(dom + block - REACH + n_dom, n_dom), me),
            device_id_type=MESH_ID,
        )

    base_copy = pltpu.make_async_copy(base_ref, base_in.at[pl.ds(LEAD, BASE_ROWS)], base_sem)
    base_copy.start()

    def out_copy(step, distance):
        peer = lax.rem(me + distance, PLANE)
        return pltpu.make_async_remote_copy(
            src_ref=send_out.at[step, pl.ds(pl.multiple_of(peer * WIRE, 8), WIRE)],
            dst_ref=recv_out.at[step, pl.ds(pl.multiple_of(me * WIRE, 8), WIRE)],
            send_sem=out_send.at[step, distance - 1],
            recv_sem=out_recv.at[step, distance - 1],
            device_id=(dom, peer),
            device_id_type=MESH_ID,
        )

    def back_copy(step, distance):
        peer = lax.rem(me + distance, PLANE)
        return pltpu.make_async_remote_copy(
            src_ref=send_back.at[step, pl.ds(pl.multiple_of(peer * BACK, 8), BACK)],
            dst_ref=recv_back.at[step, pl.ds(pl.multiple_of(me * BACK, 8), BACK)],
            send_sem=back_send.at[step, distance - 1],
            recv_sem=back_recv.at[step, distance - 1],
            device_id=(dom, peer),
            device_id_type=MESH_ID,
        )

    def edge_copy(step, block):
        return pltpu.make_async_remote_copy(
            src_ref=edge_out.at[step, pl.ds(block * CAP, CAP)],
            dst_ref=edge_in.at[step, pl.ds((2 * REACH - block) * CAP, CAP)],
            send_sem=edge_send.at[step, block],
            recv_sem=edge_recv.at[step, block],
            device_id=(lax.rem(dom + block - REACH + n_dom, n_dom), me),
            device_id_type=MESH_ID,
        )

    def each_peer(what):
        def body(distance, carry):
            what(distance)
            return carry

        lax.fori_loop(1, PLANE, body, 0)

    rows_ref = adj_ref
    for comp in range(3):
        for mode in range(LOCAL):
            state[comp, 0:NPTS, ELEMS * mode : ELEMS * (mode + 1)] = rows_ref[comp, :, mode, :]
        state[comp, NPTS:KROWS, :] = jnp.zeros((KROWS - NPTS, 128), F32)
    for row in range(4):
        for group in range(4):
            metrics[row : row + 1, ELEMS * group : ELEMS * (group + 1)] = met_ref[row : row + 1, :]
    xi_x, xi_y = metrics[0:1, :], metrics[1:2, :]
    eta_x, eta_y = metrics[2:3, :], metrics[3:4, :]

    lane_row = lax.broadcasted_iota(jnp.int32, (1, 128), 1)
    wave = ((LOCAL * me + lane_row // ELEMS + 1) // 2).astype(F32)

    def send_state(step):
        rhs = three(jnp.concatenate([state[0], state[1], state[2]], axis=1))
        first = dot(deriv_ref[0 : 2 * ROWS, :], rhs)
        for comp in range(3):
            lanes = slice(128 * comp, 128 * comp + 128)
            along_xi, along_eta = first[0:ROWS, lanes], first[ROWS : 2 * ROWS, lanes]
            grads[comp, 0:ROWS, :] = xi_x * along_xi + eta_x * along_eta
            grads[3 + comp, 0:ROWS, :] = xi_y * along_xi + eta_y * along_eta

        def nodes(which):
            if which is None:
                return jnp.zeros((PLANE, 128), F32)
            field, k = which
            rows = pl.ds(k, PLANE, stride=5)
            return state[field, rows, :] if field < 3 else grads[field - 3, rows, :]

        for at, block in enumerate(OUT_BLOCKS):
            for mode, rows in enumerate(swap_blocks([nodes(which) for which in block])):
                send_out[step, pl.ds(at * 4 + mode, PLANE, stride=WIRE), :] = rows
        if step == 0:
            pl.semaphore_wait(barrier, PLANE - 1 + len(others))
        each_peer(lambda distance: out_copy(step, distance).start())
        mine = pl.ds(pl.multiple_of(me * WIRE, 8), WIRE)
        recv_out[step, mine, :] = send_out[step, mine, :]

        second = dot(deriv_ref[2 * ROWS : 5 * ROWS, :], rhs)
        diffuse = STEP_SIZE * VISCOSITY
        keep = 1.0 - diffuse * (wave * wave)
        both_xi = diffuse * (xi_x * xi_x + xi_y * xi_y)
        mixed = (2.0 * diffuse) * (xi_x * eta_x + xi_y * eta_y)
        both_eta = diffuse * (eta_x * eta_x + eta_y * eta_y)
        for comp in range(3):
            lanes = slice(128 * comp, 128 * comp + 128)
            state[comp, 0:ROWS, :] = keep * state[comp, 0:ROWS, :] + (
                both_xi * second[0:ROWS, lanes]
                + mixed * second[ROWS : 2 * ROWS, lanes]
                + both_eta * second[2 * ROWS : 3 * ROWS, lanes]
            )

    def arrange_base():
        base_in[0:LEAD, :] = jnp.zeros((LEAD, 128), F32)
        base_in[LEAD + BASE_ROWS :, :] = jnp.zeros((LEAD, 128), F32)
        base_copy.wait()
        lane = lax.broadcasted_iota(jnp.int32, (12, 128), 1)
        in_head = lane >= 2 * me
        in_tail = lane < 2 * me + (SPAN_PTS - 128)

        def body(n, carry):
            start = SPAN_PTS * n - 2 * me + 128
            block = start // 128
            shift = start - 128 * block
            back = lax.rem(128 - shift, 128)
            early = lane < 128 - shift
            for step in range(STEPS):
                rolled = []
                for at in range(3):
                    row = LEAD + STEPS * (block - 1 + at) + step
                    rows = base_in[pl.ds(row, 12, stride=STEPS * NPTS), :]
                    rolled.append(pltpu.roll(rows, back, 1))
                to = pl.ds(n, 12, stride=MODES)
                base_head[step, to, :] = jnp.where(
                    in_head, jnp.where(early, rolled[0], rolled[1]), 0.0
                )
                base_tail[step, to, :] = jnp.where(
                    in_tail, jnp.where(early, rolled[1], rolled[2]), 0.0
                )
            return carry

        lax.fori_loop(0, MODES, body, 0)

    def prepare_edges():
        slot_ids[...] = jnp.full((16, 128), -1, jnp.int32)
        for block in range(2 * REACH + 1):
            lanes = slice(CAP * block, CAP * (block + 1))
            slot_ids[0:1, lanes] = edge_ref[block : block + 1, :]
            slot_ids[8:9, lanes] = flip_ref[block : block + 1, :]
        own, flip = slot_ids[0:1, :], slot_ids[8:9, :]
        odd = lane_row % 2 == 1
        paired = jnp.where(odd, pltpu.roll(own, 1, 1), pltpu.roll(own, 127, 1))
        inner = (lane_row >= CAP * REACH) & (lane_row < CAP * (REACH + 1))
        given = jnp.where(inner, paired, own)
        edge_row = lax.broadcasted_iota(jnp.int32, (128, 128), 0)
        hot = jnp.where(edge_row == own, 1.0, 0.0).astype(F32)
        recv_hot[:, 0:128] = hot.astype(BF16)
        recv_hot[:, 128:256] = hot.astype(BF16)
        gave = jnp.where(edge_row == given, 1.0, 0.0).astype(F32)
        turned = jnp.where(flip == 1, gave, 0.0)
        straight = (gave - turned).T.astype(BF16)
        turned = turned.T.astype(BF16)
        for part in range(2):
            send_hot[:, 256 * part : 256 * part + 128] = straight
            send_hot[:, 256 * part + 128 : 256 * part + 256] = turned
        counts = jnp.sum(hot.T, axis=0, keepdims=True)
        spread = []
        for edge in range(4):
            one = jnp.where(lane_row // ELEMS == edge, counts, 0.0)
            one = one + pltpu.roll(one, 64, 1)
            spread.append(one + pltpu.roll(one, 32, 1))
        inv_weight[...] = jnp.ones((KROWS, 128), F32)
        first_col, last_col = pl.ds(0, NODES, stride=NODES), pl.ds(8, NODES, stride=NODES)
        for rows, edge in ((first_col, 0), (slice(72, 81), 1), (last_col, 2), (slice(0, 9), 3)):
            inv_weight[rows, :] = inv_weight[rows, :] + spread[edge]
        inv_weight[...] = 1.0 / inv_weight[...]
        trace_b[...] = jnp.zeros((128, 256), F32)

    def physical(step):
        each_peer(lambda distance: out_copy(step, distance).wait_recv())
        columns = []
        for at in range(len(OUT_BLOCKS)):
            columns.append(
                jnp.concatenate(
                    [
                        recv_out[step, pl.ds(at * 4 + mode, PLANE, stride=WIRE), :]
                        for mode in range(LOCAL)
                    ],
                    axis=0,
                )
            )
        state_rhs = three(jnp.concatenate(columns[:STATE_BLOCKS], axis=1))
        grad_rhs = three(jnp.concatenate(columns[STATE_BLOCKS:], axis=1))
        of_state = dot(span_ref[...], state_rhs)
        of_grads = dot(span_ref[0:MODES, :], grad_rhs)

        def block_of(at, slope):
            if at < STATE_BLOCKS:
                rows = slice(MODES, 2 * MODES) if slope else slice(0, MODES)
                return of_state[rows, 128 * at : 128 * at + 128]
            at = at - STATE_BLOCKS
            return of_grads[:, 128 * at : 128 * at + 128]

        def head_of(field, slope=False):
            return block_of(HEAD_AT[field], slope)

        def tail_of(field, slope=False):
            at, side = TAIL_AT[field]
            both = block_of(at, slope)
            return pltpu.roll(both, 64, 1) if side else both

        def products(values, base):
            def flow(index):
                return base[step, MODES * index : MODES * (index + 1), :]

            state_now = [values(i) for i in range(3)]
            results = []
            for comp in range(3):
                term = (
                    flow(0) * values(3 + comp)
                    + flow(1) * values(6 + comp)
                    + flow(2) * values(comp, True)
                )
                results.append(
                    term
                    - (
                        state_now[0] * flow(3 + comp)
                        + state_now[1] * flow(6 + comp)
                        + state_now[2] * flow(9 + comp)
                    )
                )
            return results

        heads = products(head_of, base_head)
        tails = products(tail_of, base_tail)
        packed = heads + [tails[0] + pltpu.roll(tails[1], 64, 1), tails[2]]
        back = dot(fwd_ref[...], three(jnp.concatenate(packed, axis=1)))
        for at in range(5):
            for mode in range(LOCAL):
                send_back[step, pl.ds(at * 4 + mode, PLANE, stride=BACK), :] = back[
                    PLANE * mode : PLANE * (mode + 1), 128 * at : 128 * at + 128
                ]
        for mode in range(LOCAL):
            send_back[step, pl.ds(20 + mode, PLANE, stride=BACK), :] = jnp.zeros((PLANE, 128), F32)
        each_peer(lambda distance: back_copy(step, distance).start())
        mine = pl.ds(pl.multiple_of(me * BACK, 8), BACK)
        recv_back[step, mine, :] = send_back[step, mine, :]

    def update(step):
        each_peer(lambda distance: back_copy(step, distance).wait_recv())
        blocks = []
        for at in range(5):
            blocks.append(
                swap_blocks(
                    [
                        recv_back[step, pl.ds(at * 4 + mode, PLANE, stride=BACK), :]
                        for mode in range(LOCAL)
                    ]
                )
            )
        for comp in range(3):
            ends = blocks[3 + comp // 2][2 * (comp % 2) : 2 * (comp % 2) + 2]
            for k, rate in enumerate(blocks[comp] + ends):
                rows = pl.ds(k, PLANE, stride=5)
                state[comp, rows, :] = state[comp, rows, :] + STEP_SIZE * rate

    def exchange(step):
        first_col, last_col = pl.ds(0, NODES, stride=NODES), pl.ds(8, NODES, stride=NODES)
        edge_rows = (first_col, slice(72, 81), last_col, slice(0, 9))
        for comp in range(3):
            traces = swap_blocks([state[comp, rows, :] for rows in edge_rows])
            for mode in range(LOCAL):
                at = (comp * LOCAL + mode) * 16
                trace_a[at : at + NODES, :] = traces[mode]
        for i in range(NODES):
            rows = trace_a[pl.ds(i, 3 * LOCAL, stride=16), :]
            trace_b[12 * i : 12 * i + 12, 0:128] = rows
            trace_b[12 * (8 - i) : 12 * (8 - i) + 12, 128:256] = rows
        hi, lo = halves(trace_b[...])
        given = lax.dot_general(
            send_hot[...],
            jnp.concatenate([hi, lo], axis=1),
            (((1,), (1,)), ((), ())),
            preferred_element_type=F32,
        )
        edge_out[step] = given
        for block in others:
            edge_copy(step, block).start()
        inner = slice(CAP * REACH, CAP * (REACH + 1))
        edge_in[step, inner, :] = given[inner, :]
        edge_in[step, 120:128, :] = jnp.zeros((8, 128), F32)
        for block in others:
            edge_copy(step, block).wait_recv()
        hi, lo = halves(edge_in[step])
        sums[...] = dot(recv_hot[...], jnp.concatenate([hi, lo], axis=0)).T
        for comp in range(3):
            parts = swap_blocks(
                [sums[pl.ds(comp * LOCAL + mode, NODES, stride=12), :] for mode in range(LOCAL)]
            )
            for rows, part in zip(edge_rows, parts):
                state[comp, rows, :] = state[comp, rows, :] + part
            state[comp, 0:ROWS, :] = state[comp, 0:ROWS, :] * inv_weight[0:ROWS, :]

    for step in range(STEPS):
        send_state(step)
        if step == 0:
            prepare_edges()
            arrange_base()
        physical(step)
        update(step)
        exchange(step)

    for comp in range(3):
        for mode in range(LOCAL):
            out_ref[comp, :, mode, :] = state[comp, 0:NPTS, ELEMS * mode : ELEMS * (mode + 1)]

    for step in range(STEPS):
        each_peer(lambda distance, step=step: out_copy(step, distance).wait_send())
        each_peer(lambda distance, step=step: back_copy(step, distance).wait_send())
        for block in others:
            edge_copy(step, block).wait_send()


def shards(n_dom, adjoint, metric, base_flow, edge_list, flips):
    state_in = jnp.transpose(adjoint, (0, 2, 3, 1, 4)).reshape(3, NPTS, LOCAL, ELEMS)
    base_in = (
        base_flow.reshape(STEPS, 12, NPTS, 128).transpose(1, 2, 0, 3).reshape(BASE_ROWS, 128)
    )
    span, fwd = span_tables()
    vmem = pl.BlockSpec(memory_space=pltpu.VMEM)
    dma = pltpu.SemaphoreType.DMA
    result = pl.pallas_call(
        functools.partial(kernel, n_dom),
        out_shape=jax.ShapeDtypeStruct((3, NPTS, LOCAL, ELEMS), F32),
        in_specs=[vmem, vmem, pl.BlockSpec(memory_space=pl.ANY)] + [vmem] * 5,
        out_specs=vmem,
        scratch_shapes=[
            pltpu.VMEM((3, KROWS, 128), F32),
            pltpu.VMEM((6, KROWS, 128), F32),
            pltpu.VMEM((BASE_ROWS + 2 * LEAD, 128), F32),
            pltpu.VMEM((STEPS, 12 * MODES, 128), F32),
            pltpu.VMEM((STEPS, 12 * MODES, 128), F32),
            pltpu.VMEM((STEPS, PLANE * WIRE, 128), F32),
            pltpu.VMEM((STEPS, PLANE * WIRE, 128), F32),
            pltpu.VMEM((STEPS, PLANE * BACK, 128), F32),
            pltpu.VMEM((STEPS, PLANE * BACK, 128), F32),
            pltpu.VMEM((STEPS, 128, 128), F32),
            pltpu.VMEM((STEPS, 128, 128), F32),
            pltpu.VMEM((3 * LOCAL * 16, 128), F32),
            pltpu.VMEM((128, 256), F32),
            pltpu.VMEM((128, 128), F32),
            pltpu.VMEM((128, 512), BF16),
            pltpu.VMEM((128, 256), BF16),
            pltpu.VMEM((KROWS, 128), F32),
            pltpu.VMEM((8, 128), F32),
            pltpu.VMEM((16, 128), jnp.int32),
            dma(()),
            dma((STEPS, PLANE - 1)),
            dma((STEPS, PLANE - 1)),
            dma((STEPS, PLANE - 1)),
            dma((STEPS, PLANE - 1)),
            dma((STEPS, 2 * REACH + 1)),
            dma((STEPS, 2 * REACH + 1)),
        ],
        compiler_params=pltpu.CompilerParams(
            collective_id=0, has_side_effects=True, vmem_limit_bytes=40 * 1024 * 1024
        ),
    )(
        state_in,
        metric,
        base_in,
        edge_list[0],
        flips[0],
        jnp.asarray(derivative_tables()),
        jnp.asarray(span),
        jnp.asarray(fwd),
    )
    return jnp.transpose(result.reshape(3, NODES, NODES, LOCAL, ELEMS), (0, 3, 1, 2, 4))


def solution(mesh):
    placed = (
        P(None, "plane", None, None, "dom"),
        P(None, "dom"),
        P(None, None, ("dom", "plane")),
        P("dom", None, None),
        P("dom", None, None),
    )
    return jax.shard_map(
        functools.partial(shards, mesh.shape["dom"]),
        mesh=mesh,
        in_specs=placed,
        out_specs=P(None, "plane", None, None, "dom"),
        check_vma=False,
    )
```

profile of v0, /device:TPU:1, one launch (start us, length us, event | category | flops | bytes accessed | tf_op | source)
XLA Modules:
  0.0 71.8 jit_solution(6827839351502129942)
XLA Ops:
  0.0 2.0 %reshape.13 = f32[2,12,81,128]{3,2,0,1:T(8,128)S(1)} reshape(f32[2,12,10368]{2,0,1:T(2,128)} %param.10) | data formatting | bytes 1990656 | tf_op jit(solution)/shard_map/reshape | solution.py:508
  2.0 0.0 copy-start.5
  2.0 0.0 copy-start.6
  2.0 0.0 copy-start
  2.0 0.0 copy-start.1
  2.1 0.0 copy-start.2
  2.1 0.0 copy-start.3
  2.1 0.0 copy-start.4
  2.1 0.5 copy.10
  2.6 0.1 copy-done.5
  2.7 0.0 copy-done.6
  2.7 0.4 copy-done
  3.1 0.1 copy-done.1
  3.2 0.0 copy-done.2
  3.2 0.0 copy-done.3
  3.2 0.0 copy-done.4
  3.2 67.8 %shard_map.82 = f32[3,81,4,32]{3,2,1,0:T(4,128)S(1)} custom-call(f32[3,81,4,32]{3,2,1,0:T(4,128)S(1)} %bitcast.16, f32[4,32]{1,0:T(4,128)S(1)} %copy-done.4, f32[1944,128]{1,0:T(8,128)S(1)} %bitcast.14, s32[5,24]{1,0:T(8,128)S(1)} %get-tuple-element.6.edge_ref, s32[5,24]{1,0:T(8,128)S(1)} %get-tuple-element.5.flip_ref, bf16[440,288]{1,0:T(8,128)(2,1)S(1)} %copy-done.1, ...), custom_call_target="tpu_custom_call" | custom-call | tf_op jit(solution)/shard_map/pallas_call | solution.py:513
  71.0 0.8 %copy.16 = f32[3,4,9,9,32]{4,1,3,2,0:T(4,128)} copy(f32[3,4,9,9,32]{4,1,3,2,0:T(4,128)S(1)} %bitcast.15) | data formatting | bytes 248832
  (1 shorter events, 0.0 us)
Async XLA Ops:
  2.0 0.7 copy-start.5
  2.0 0.7 copy-start.6
  2.0 1.0 %copy-start = (f32[3,4,9,9,32]{4,1,3,2,0:T(4,128)S(1)}, f32[3,4,9,9,32]{4,1,3,2,0:T(4,128)}, u32[]{:S(2)}) copy-start(f32[3,4,9,9,32]{4,1,3,2,0:T(4,128)} %param.8) | copy-start | bytes 373252
  2.0 1.1 %copy-start.1 = (bf16[440,288]{1,0:T(8,128)(2,1)S(1)}, bf16[440,288]{1,0:T(8,128)(2,1)}, u32[]{:S(2)}) copy-start(bf16[440,288]{1,0:T(8,128)(2,1)} %constant.6.clone.deriv_ref) | copy-start | bytes 760324
  2.1 1.1 %copy-start.2 = (bf16[128,192]{1,0:T(8,128)(2,1)S(1)}, bf16[128,192]{1,0:T(8,128)(2,1)}, u32[]{:S(2)}) copy-start(bf16[128,192]{1,0:T(8,128)(2,1)} %constant.7.clone.span_ref) | copy-start | bytes 147460
  2.1 1.1 %copy-start.3 = (bf16[64,192]{1,0:T(8,128)(2,1)S(1)}, bf16[64,192]{1,0:T(8,128)(2,1)}, u32[]{:S(2)}) copy-start(bf16[64,192]{1,0:T(8,128)(2,1)} %constant.8.clone.fwd_ref) | copy-start | bytes 73732
  2.1 1.1 %copy-start.4 = (f32[4,32]{1,0:T(4,128)S(1)}, f32[4,32]{1,0:T(4,128)}, u32[]{:S(2)}) copy-start(f32[4,32]{1,0:T(4,128)} %met_ref.1) | copy-start | bytes 1540
where the time goes:
time: 72 us; the launch traced here: 71.8 us
  Pallas kernels  67.8 us (94%)
  local copies, waits for them, and re-layouts  3.89 us (5%)
    pallas_call x1, Pallas kernels, shards(): pl.pallas_call(functools.partial(kernel, n_dom), out_shape=jax.ShapeDtype...  67.8 us
    reshape x1, local copies, waits for them, and re-layouts, shards(): base_flow.reshape(STEPS, 12, NPTS, 128).transpose(1, 2, 0, 3)  2 us

commit v1 on v0

--- a/solution.py
+++ b/solution.py
@@ -24,10 +24,10 @@
 
 ROWS = 88
 KROWS = 96
-WIRE = 56
-BACK = 24
-LEAD = 8
-BASE_ROWS = 12 * NPTS * STEPS
+WIRE = 48
+BACK = 16
+REST = SPAN_PTS - 128
+FLOWS = 12 * STEPS
 
 F32 = jnp.float32
 BF16 = jnp.bfloat16
@@ -118,23 +118,14 @@
     return [c0, c1, c2, c3]
 
 
-def head(field):
-    return [(field, k) for k in range(4)]
-
-
-def tail(first, second):
-    pair = [(first, 4), (first, 5)]
-    return pair + ([(second, 4), (second, 5)] if second is not None else [None, None])
-
-
-OUT_BLOCKS = (
-    [head(0), head(1), head(2), tail(0, 1), tail(2, 3)]
-    + [head(3), head(4), head(5), head(6), head(7), head(8)]
-    + [tail(4, 5), tail(6, 7), tail(8, None)]
-)
-STATE_BLOCKS = 5
-HEAD_AT = {0: 0, 1: 1, 2: 2, 3: 5, 4: 6, 5: 7, 6: 8, 7: 9, 8: 10}
-TAIL_AT = {0: (3, 0), 1: (3, 1), 2: (4, 0), 3: (4, 1), 4: (11, 0), 5: (11, 1), 6: (12, 0), 7: (12, 1), 8: (13, 0)}
+def turn(x, shift):
+    return pltpu.roll(x, shift % 128, 1) if shift % 128 else x
+
+
+STATE_BLOCKS = 4
+HEAD_AT = (0, 1, 2, 4, 5, 6, 7, 8, 9)
+TAIL_AT = (3, 10, 11)
+DISTANCES = (8, 7, 9, 6, 10, 5, 11, 4, 12, 3, 13, 2, 14, 1, 15)
 
 
 def kernel(
@@ -151,6 +142,7 @@
     state,
     grads,
     base_in,
+    base_rows,
     base_head,
     base_tail,
     send_out,
@@ -167,7 +159,14 @@
     inv_weight,
     metrics,
     slot_ids,
-    base_sem,
+    adj_in,
+    met_in,
+    deriv_in,
+    edge_ids,
+    flip_ids,
+    span_in,
+    fwd_in,
+    load_sem,
     out_send,
     out_recv,
     back_send,
@@ -196,8 +195,21 @@
             device_id_type=MESH_ID,
         )
 
-    base_copy = pltpu.make_async_copy(base_ref, base_in.at[pl.ds(LEAD, BASE_ROWS)], base_sem)
-    base_copy.start()
+    loads = {}
+    for at, (name, source, target) in enumerate(
+        (
+            ("state", adj_ref, adj_in),
+            ("metric", met_ref, met_in),
+            ("deriv", deriv_ref, deriv_in),
+            ("base", base_ref, base_in),
+            ("edges", edge_ref, edge_ids),
+            ("flips", flip_ref, flip_ids),
+            ("span", span_ref, span_in),
+            ("forward", fwd_ref, fwd_in),
+        )
+    ):
+        loads[name] = pltpu.make_async_copy(source, target, load_sem.at[at])
+        loads[name].start()
 
     def out_copy(step, distance):
         peer = lax.rem(me + distance, PLANE)
@@ -232,52 +244,78 @@
         )
 
     def each_peer(what):
-        def body(distance, carry):
+        for distance in DISTANCES:
             what(distance)
-            return carry
-
-        lax.fori_loop(1, PLANE, body, 0)
-
-    rows_ref = adj_ref
+
+    loads["state"].wait()
     for comp in range(3):
         for mode in range(LOCAL):
-            state[comp, 0:NPTS, ELEMS * mode : ELEMS * (mode + 1)] = rows_ref[comp, :, mode, :]
+            state[comp, 0:NPTS, ELEMS * mode : ELEMS * (mode + 1)] = adj_in[comp, :, mode, :]
         state[comp, NPTS:KROWS, :] = jnp.zeros((KROWS - NPTS, 128), F32)
+    loads["metric"].wait()
     for row in range(4):
         for group in range(4):
-            metrics[row : row + 1, ELEMS * group : ELEMS * (group + 1)] = met_ref[row : row + 1, :]
+            metrics[row : row + 1, ELEMS * group : ELEMS * (group + 1)] = met_in[row : row + 1, :]
     xi_x, xi_y = metrics[0:1, :], metrics[1:2, :]
     eta_x, eta_y = metrics[2:3, :], metrics[3:4, :]
 
     lane_row = lax.broadcasted_iota(jnp.int32, (1, 128), 1)
+    owner_lane = lax.broadcasted_iota(jnp.int32, (PLANE, 128), 1)
+    owner_start = 2 * lax.broadcasted_iota(jnp.int32, (PLANE, 128), 0)
+    after = owner_lane >= owner_start
+    places = []
+    for comp in range(3):
+        place = (owner_lane - owner_start + (128 - REST * comp)) % 128
+        places.append(place < REST)
     wave = ((LOCAL * me + lane_row // ELEMS + 1) // 2).astype(F32)
 
     def send_state(step):
         rhs = three(jnp.concatenate([state[0], state[1], state[2]], axis=1))
-        first = dot(deriv_ref[0 : 2 * ROWS, :], rhs)
+        if step == 0:
+            loads["deriv"].wait()
+        first = dot(deriv_in[0 : 2 * ROWS, :], rhs)
         for comp in range(3):
             lanes = slice(128 * comp, 128 * comp + 128)
             along_xi, along_eta = first[0:ROWS, lanes], first[ROWS : 2 * ROWS, lanes]
             grads[comp, 0:ROWS, :] = xi_x * along_xi + eta_x * along_eta
             grads[3 + comp, 0:ROWS, :] = xi_y * along_xi + eta_y * along_eta
 
-        def nodes(which):
-            if which is None:
-                return jnp.zeros((PLANE, 128), F32)
-            field, k = which
+        def nodes(field, k):
             rows = pl.ds(k, PLANE, stride=5)
             return state[field, rows, :] if field < 3 else grads[field - 3, rows, :]
 
-        for at, block in enumerate(OUT_BLOCKS):
-            for mode, rows in enumerate(swap_blocks([nodes(which) for which in block])):
-                send_out[step, pl.ds(at * 4 + mode, PLANE, stride=WIRE), :] = rows
+        zeros = jnp.zeros((PLANE, 128), F32)
+
+        def ends(first, second):
+            parts = [nodes(first, 4), nodes(first, 5)]
+            parts += [zeros, zeros] if second is None else [nodes(second, 4), nodes(second, 5)]
+            return swap_blocks(parts)
+
+        def put(at, mode, rows):
+            send_out[step, pl.ds(at * 4 + mode, PLANE, stride=WIRE), :] = rows
+
+        for group in range(3):
+            fields = [3 * group + comp for comp in range(3)]
+            early, late = ends(fields[0], fields[1]), ends(fields[2], None)
+            packed = [zeros] * LOCAL
+            for comp, field in enumerate(fields):
+                heads = swap_blocks([nodes(field, k) for k in range(4)])
+                both, side = (late, 0) if comp == 2 else (early, 64 * comp)
+                for mode in range(LOCAL):
+                    late_points = turn(both[mode], -side)
+                    put(HEAD_AT[field], mode, jnp.where(after, heads[mode], late_points))
+                    packed[mode] = jnp.where(
+                        places[comp], turn(both[mode], REST * comp - side), packed[mode]
+                    )
+            for mode in range(LOCAL):
+                put(TAIL_AT[group], mode, packed[mode])
         if step == 0:
             pl.semaphore_wait(barrier, PLANE - 1 + len(others))
         each_peer(lambda distance: out_copy(step, distance).start())
         mine = pl.ds(pl.multiple_of(me * WIRE, 8), WIRE)
         recv_out[step, mine, :] = send_out[step, mine, :]
 
-        second = dot(deriv_ref[2 * ROWS : 5 * ROWS, :], rhs)
+        second = dot(deriv_in[2 * ROWS : 5 * ROWS, :], rhs)
         diffuse = STEP_SIZE * VISCOSITY
         keep = 1.0 - diffuse * (wave * wave)
         both_xi = diffuse * (xi_x * xi_x + xi_y * xi_y)
@@ -292,42 +330,46 @@
             )
 
     def arrange_base():
-        base_in[0:LEAD, :] = jnp.zeros((LEAD, 128), F32)
-        base_in[LEAD + BASE_ROWS :, :] = jnp.zeros((LEAD, 128), F32)
-        base_copy.wait()
-        lane = lax.broadcasted_iota(jnp.int32, (12, 128), 1)
-        in_head = lane >= 2 * me
-        in_tail = lane < 2 * me + (SPAN_PTS - 128)
+        loads["base"].wait()
+
+        def gather(block, carry):
+            lanes = pl.ds(pl.multiple_of(128 * block, 128), 128)
+            rows = pl.ds(pl.multiple_of(FLOWS * block, 8), FLOWS)
+            base_rows[rows, :] = base_in[:, :, lanes].reshape(FLOWS, 128)
+            return carry
+
+        lax.fori_loop(0, NPTS, gather, 0)
+        base_rows[FLOWS * NPTS :, :] = jnp.zeros((2 * FLOWS, 128), F32)
+        lane = lax.broadcasted_iota(jnp.int32, (FLOWS, 128), 1)
+        point = (lane - 2 * me + 128) % 128
 
         def body(n, carry):
-            start = SPAN_PTS * n - 2 * me + 128
+            start = SPAN_PTS * n
             block = start // 128
             shift = start - 128 * block
-            back = lax.rem(128 - shift, 128)
-            early = lane < 128 - shift
-            for step in range(STEPS):
-                rolled = []
-                for at in range(3):
-                    row = LEAD + STEPS * (block - 1 + at) + step
-                    rows = base_in[pl.ds(row, 12, stride=STEPS * NPTS), :]
-                    rolled.append(pltpu.roll(rows, back, 1))
-                to = pl.ds(n, 12, stride=MODES)
-                base_head[step, to, :] = jnp.where(
-                    in_head, jnp.where(early, rolled[0], rolled[1]), 0.0
-                )
-                base_tail[step, to, :] = jnp.where(
-                    in_tail, jnp.where(early, rolled[1], rolled[2]), 0.0
-                )
+            back = lax.rem(128 - shift + 2 * me, 128)
+            early = point < 128 - shift
+            rolled = []
+            for at in range(3):
+                rows = pl.ds(pl.multiple_of(FLOWS * (block + at), 8), FLOWS)
+                rolled.append(pltpu.roll(base_rows[rows, :], back, 1))
+            to = pl.ds(n, FLOWS, stride=MODES)
+            base_head[to, :] = jnp.where(early, rolled[0], rolled[1])
+            base_tail[to, :] = jnp.where(
+                point < REST, jnp.where(early, rolled[1], rolled[2]), 0.0
+            )
             return carry
 
         lax.fori_loop(0, MODES, body, 0)
 
     def prepare_edges():
+        loads["edges"].wait()
+        loads["flips"].wait()
         slot_ids[...] = jnp.full((16, 128), -1, jnp.int32)
         for block in range(2 * REACH + 1):
             lanes = slice(CAP * block, CAP * (block + 1))
-            slot_ids[0:1, lanes] = edge_ref[block : block + 1, :]
-            slot_ids[8:9, lanes] = flip_ref[block : block + 1, :]
+            slot_ids[0:1, lanes] = edge_ids[block]
+            slot_ids[8:9, lanes] = flip_ids[block]
         own, flip = slot_ids[0:1, :], slot_ids[8:9, :]
         odd = lane_row % 2 == 1
         paired = jnp.where(odd, pltpu.roll(own, 1, 1), pltpu.roll(own, 127, 1))
@@ -360,7 +402,7 @@
     def physical(step):
         each_peer(lambda distance: out_copy(step, distance).wait_recv())
         columns = []
-        for at in range(len(OUT_BLOCKS)):
+        for at in range(WIRE // LOCAL):
             columns.append(
                 jnp.concatenate(
                     [
@@ -372,8 +414,11 @@
             )
         state_rhs = three(jnp.concatenate(columns[:STATE_BLOCKS], axis=1))
         grad_rhs = three(jnp.concatenate(columns[STATE_BLOCKS:], axis=1))
-        of_state = dot(span_ref[...], state_rhs)
-        of_grads = dot(span_ref[0:MODES, :], grad_rhs)
+        if step == 0:
+            loads["span"].wait()
+            loads["forward"].wait()
+        of_state = dot(span_in[...], state_rhs)
+        of_grads = dot(span_in[0:MODES, :], grad_rhs)
 
         def block_of(at, slope):
             if at < STATE_BLOCKS:
@@ -386,13 +431,14 @@
             return block_of(HEAD_AT[field], slope)
 
         def tail_of(field, slope=False):
-            at, side = TAIL_AT[field]
-            both = block_of(at, slope)
-            return pltpu.roll(both, 64, 1) if side else both
+            packed = block_of(TAIL_AT[field // 3], slope)
+            place = REST * (field % 3)
+            return pltpu.roll(packed, 128 - place, 1) if place else packed
 
         def products(values, base):
             def flow(index):
-                return base[step, MODES * index : MODES * (index + 1), :]
+                row = MODES * (STEPS * index + step)
+                return base[row : row + MODES, :]
 
             state_now = [values(i) for i in range(3)]
             results = []
@@ -414,34 +460,39 @@
 
         heads = products(head_of, base_head)
         tails = products(tail_of, base_tail)
-        packed = heads + [tails[0] + pltpu.roll(tails[1], 64, 1), tails[2]]
-        back = dot(fwd_ref[...], three(jnp.concatenate(packed, axis=1)))
-        for at in range(5):
+        rest = tails[0] + pltpu.roll(tails[1], REST, 1) + pltpu.roll(tails[2], 2 * REST, 1)
+        packed = heads + [rest]
+        back = dot(fwd_in[...], three(jnp.concatenate(packed, axis=1)))
+        for at in range(4):
             for mode in range(LOCAL):
                 send_back[step, pl.ds(at * 4 + mode, PLANE, stride=BACK), :] = back[
                     PLANE * mode : PLANE * (mode + 1), 128 * at : 128 * at + 128
                 ]
-        for mode in range(LOCAL):
-            send_back[step, pl.ds(20 + mode, PLANE, stride=BACK), :] = jnp.zeros((PLANE, 128), F32)
         each_peer(lambda distance: back_copy(step, distance).start())
         mine = pl.ds(pl.multiple_of(me * BACK, 8), BACK)
         recv_back[step, mine, :] = send_back[step, mine, :]
 
     def update(step):
         each_peer(lambda distance: back_copy(step, distance).wait_recv())
-        blocks = []
-        for at in range(5):
-            blocks.append(
-                swap_blocks(
-                    [
-                        recv_back[step, pl.ds(at * 4 + mode, PLANE, stride=BACK), :]
-                        for mode in range(LOCAL)
-                    ]
-                )
-            )
+        def came(at, mode):
+            return recv_back[step, pl.ds(at * 4 + mode, PLANE, stride=BACK), :]
+
+        rest = [came(3, mode) for mode in range(LOCAL)]
+        heads, ends = [], []
         for comp in range(3):
-            ends = blocks[3 + comp // 2][2 * (comp % 2) : 2 * (comp % 2) + 2]
-            for k, rate in enumerate(blocks[comp] + ends):
+            firsts, lasts = [], []
+            for mode in range(LOCAL):
+                moved = came(comp, mode)
+                last = jnp.where(places[0], turn(rest[mode], -REST * comp), 0.0)
+                firsts.append(jnp.where(after, moved, 0.0))
+                lasts.append(jnp.where(after, last, moved))
+            heads.append(swap_blocks(firsts))
+            ends.append(lasts)
+        joined = [jnp.where(owner_lane < 64, x, pltpu.roll(y, 64, 1)) for x, y in zip(*ends[:2])]
+        early, late = swap_blocks(joined), swap_blocks(ends[2])
+        ends = (early[:2], early[2:], late[:2])
+        for comp in range(3):
+            for k, rate in enumerate(heads[comp] + ends[comp]):
                 rows = pl.ds(k, PLANE, stride=5)
                 state[comp, rows, :] = state[comp, rows, :] + STEP_SIZE * rate
 
@@ -504,23 +555,23 @@
 
 def shards(n_dom, adjoint, metric, base_flow, edge_list, flips):
     state_in = jnp.transpose(adjoint, (0, 2, 3, 1, 4)).reshape(3, NPTS, LOCAL, ELEMS)
-    base_in = (
-        base_flow.reshape(STEPS, 12, NPTS, 128).transpose(1, 2, 0, 3).reshape(BASE_ROWS, 128)
-    )
+    base_in = jnp.transpose(base_flow, (1, 0, 2))
+    deriv = derivative_tables()
     span, fwd = span_tables()
     vmem = pl.BlockSpec(memory_space=pltpu.VMEM)
     dma = pltpu.SemaphoreType.DMA
     result = pl.pallas_call(
         functools.partial(kernel, n_dom),
         out_shape=jax.ShapeDtypeStruct((3, NPTS, LOCAL, ELEMS), F32),
-        in_specs=[vmem, vmem, pl.BlockSpec(memory_space=pl.ANY)] + [vmem] * 5,
+        in_specs=[pl.BlockSpec(memory_space=pltpu.HBM)] * 8,
         out_specs=vmem,
         scratch_shapes=[
             pltpu.VMEM((3, KROWS, 128), F32),
             pltpu.VMEM((6, KROWS, 128), F32),
-            pltpu.VMEM((BASE_ROWS + 2 * LEAD, 128), F32),
-            pltpu.VMEM((STEPS, 12 * MODES, 128), F32),
-            pltpu.VMEM((STEPS, 12 * MODES, 128), F32),
+            pltpu.VMEM((12, STEPS, 128 * NPTS), F32),
+            pltpu.VMEM((FLOWS * (NPTS + 2), 128), F32),
+            pltpu.VMEM((FLOWS * MODES, 128), F32),
+            pltpu.VMEM((FLOWS * MODES, 128), F32),
             pltpu.VMEM((STEPS, PLANE * WIRE, 128), F32),
             pltpu.VMEM((STEPS, PLANE * WIRE, 128), F32),
             pltpu.VMEM((STEPS, PLANE * BACK, 128), F32),
@@ -535,7 +586,14 @@
             pltpu.VMEM((KROWS, 128), F32),
             pltpu.VMEM((8, 128), F32),
             pltpu.VMEM((16, 128), jnp.int32),
-            dma(()),
+            pltpu.VMEM((3, NPTS, LOCAL, ELEMS), F32),
+            pltpu.VMEM((4, ELEMS), F32),
+            pltpu.VMEM(deriv.shape, BF16),
+            pltpu.VMEM((2 * REACH + 1, 1, CAP), jnp.int32),
+            pltpu.VMEM((2 * REACH + 1, 1, CAP), jnp.int32),
+            pltpu.VMEM(span.shape, BF16),
+            pltpu.VMEM(fwd.shape, BF16),
+            dma((8,)),
             dma((STEPS, PLANE - 1)),
             dma((STEPS, PLANE - 1)),
             dma((STEPS, PLANE - 1)),
@@ -544,15 +602,15 @@
             dma((STEPS, 2 * REACH + 1)),
         ],
         compiler_params=pltpu.CompilerParams(
-            collective_id=0, has_side_effects=True, vmem_limit_bytes=40 * 1024 * 1024
+            collective_id=0, has_side_effects=True, vmem_limit_bytes=58 * 1024 * 1024
         ),
     )(
         state_in,
         metric,
         base_in,
-        edge_list[0],
-        flips[0],
-        jnp.asarray(derivative_tables()),
+        jnp.transpose(edge_list, (1, 0, 2)),
+        jnp.transpose(flips, (1, 0, 2)),
+        jnp.asarray(deriv),
         jnp.asarray(span),
         jnp.asarray(fwd),
     )

time: 72 us -> 62.8 us (0.87)
  Pallas kernels: 67.8 us -> 60.8 us
  local copies, waits for them, and re-layouts: 3.89 us -> 1.85 us
    pallas_call x1, Pallas kernels: 67.8 us -> 60.8 us  [shards(): pl.pallas_call(functools.partial(kernel, n_dom), out_shape=jax.ShapeDtype...]
    reshape x1 -> x0, local copies, waits for them, and re-layouts: 2 us -> none  [shards(): base_flow.reshape(STEPS, 12, NPTS, 128).transpose(1, 2, 0, 3)]
    unnamed x16 -> x1, local copies, waits for them, and re-layouts: 1.37 us -> 1.85 us
where the time goes in v1:
time: 62.8 us; the launch traced here: 62.7 us
  Pallas kernels  60.8 us (97%)
  local copies, waits for them, and re-layouts  1.85 us (3%)
    pallas_call x1, Pallas kernels, shards(): pl.pallas_call(functools.partial(kernel, n_dom), out_shape=jax.ShapeDtype...  60.8 us
    unnamed x1, local copies, waits for them, and re-layouts  1.85 us

profile of v1, /device:TPU:1, one launch (start us, length us, event | category | flops | bytes accessed | tf_op | source)
XLA Modules:
  0.0 62.7 jit_solution(9012560662883040192)
XLA Ops:
  0.0 60.8 %shard_map.82 = f32[3,81,4,32]{3,2,1,0:T(4,128)} custom-call(f32[3,81,4,32]{3,2,1,0:T(4,128)} %bitcast.11, f32[4,32]{1,0:T(4,128)} %met_ref.1, f32[12,2,10368]{2,1,0:T(2,128)} %bitcast.10, s32[5,1,24]{2,1,0:T(1,128)} %bitcast.12, s32[5,1,24]{2,1,0:T(1,128)} %bitcast.13, bf16[440,288]{1,0:T(8,128)(2,1)} %constant.6.clone.deriv_ref, ...), custom_call_target="tpu_custom_call" | custom-call | tf_op jit(solution)/shard_map/pallas_call | solution.py:563
  60.8 1.9 %copy.10 = f32[3,4,9,9,32]{4,1,3,2,0:T(4,128)} copy(f32[3,4,9,9,32]{4,1,3,2,0:T(4,128)} %bitcast.9) | data formatting | bytes 248832

commit v2 on v1

--- a/solution.py
+++ b/solution.py
@@ -216,8 +216,8 @@
         return pltpu.make_async_remote_copy(
             src_ref=send_out.at[step, pl.ds(pl.multiple_of(peer * WIRE, 8), WIRE)],
             dst_ref=recv_out.at[step, pl.ds(pl.multiple_of(me * WIRE, 8), WIRE)],
-            send_sem=out_send.at[step, distance - 1],
-            recv_sem=out_recv.at[step, distance - 1],
+            send_sem=out_send.at[step],
+            recv_sem=out_recv.at[step],
             device_id=(dom, peer),
             device_id_type=MESH_ID,
         )
@@ -227,8 +227,8 @@
         return pltpu.make_async_remote_copy(
             src_ref=send_back.at[step, pl.ds(pl.multiple_of(peer * BACK, 8), BACK)],
             dst_ref=recv_back.at[step, pl.ds(pl.multiple_of(me * BACK, 8), BACK)],
-            send_sem=back_send.at[step, distance - 1],
-            recv_sem=back_recv.at[step, distance - 1],
+            send_sem=back_send.at[step],
+            recv_sem=back_recv.at[step],
             device_id=(dom, peer),
             device_id_type=MESH_ID,
         )
@@ -240,6 +240,16 @@
             send_sem=edge_send.at[step, block],
             recv_sem=edge_recv.at[step, block],
             device_id=(lax.rem(dom + block - REACH + n_dom, n_dom), me),
+            device_id_type=MESH_ID,
+        )
+
+    def all_of(source, target, rows, send_sem, recv_sem, step):
+        return pltpu.make_async_remote_copy(
+            src_ref=source.at[step, pl.ds(0, (PLANE - 1) * rows)],
+            dst_ref=target.at[step, pl.ds(0, (PLANE - 1) * rows)],
+            send_sem=send_sem.at[step],
+            recv_sem=recv_sem.at[step],
+            device_id=(dom, lax.rem(me + 1, PLANE)),
             device_id_type=MESH_ID,
         )
 
@@ -400,7 +410,7 @@
         trace_b[...] = jnp.zeros((128, 256), F32)
 
     def physical(step):
-        each_peer(lambda distance: out_copy(step, distance).wait_recv())
+        all_of(send_out, recv_out, WIRE, out_send, out_recv, step).wait_recv()
         columns = []
         for at in range(WIRE // LOCAL):
             columns.append(
@@ -473,7 +483,7 @@
         recv_back[step, mine, :] = send_back[step, mine, :]
 
     def update(step):
-        each_peer(lambda distance: back_copy(step, distance).wait_recv())
+        all_of(send_back, recv_back, BACK, back_send, back_recv, step).wait_recv()
         def came(at, mode):
             return recv_back[step, pl.ds(at * 4 + mode, PLANE, stride=BACK), :]
 
@@ -542,15 +552,19 @@
         update(step)
         exchange(step)
 
+    out_ref[...] = state[...]
+
+    for step in range(STEPS):
+        all_of(send_out, recv_out, WIRE, out_send, out_recv, step).wait_send()
+        all_of(send_back, recv_back, BACK, back_send, back_recv, step).wait_send()
+        for block in others:
+            edge_copy(step, block).wait_send()
+
+
+def lay_out(state, out_ref):
     for comp in range(3):
         for mode in range(LOCAL):
             out_ref[comp, :, mode, :] = state[comp, 0:NPTS, ELEMS * mode : ELEMS * (mode + 1)]
-
-    for step in range(STEPS):
-        each_peer(lambda distance, step=step: out_copy(step, distance).wait_send())
-        each_peer(lambda distance, step=step: back_copy(step, distance).wait_send())
-        for block in others:
-            edge_copy(step, block).wait_send()
 
 
 def shards(n_dom, adjoint, metric, base_flow, edge_list, flips):
@@ -562,7 +576,7 @@
     dma = pltpu.SemaphoreType.DMA
     result = pl.pallas_call(
         functools.partial(kernel, n_dom),
-        out_shape=jax.ShapeDtypeStruct((3, NPTS, LOCAL, ELEMS), F32),
+        out_shape=jax.ShapeDtypeStruct((3, KROWS, 128), F32),
         in_specs=[pl.BlockSpec(memory_space=pltpu.HBM)] * 8,
         out_specs=vmem,
         scratch_shapes=[
@@ -594,10 +608,10 @@
             pltpu.VMEM(span.shape, BF16),
             pltpu.VMEM(fwd.shape, BF16),
             dma((8,)),
-            dma((STEPS, PLANE - 1)),
-            dma((STEPS, PLANE - 1)),
-            dma((STEPS, PLANE - 1)),
-            dma((STEPS, PLANE - 1)),
+            dma((STEPS,)),
+            dma((STEPS,)),
+            dma((STEPS,)),
+            dma((STEPS,)),
             dma((STEPS, 2 * REACH + 1)),
             dma((STEPS, 2 * REACH + 1)),
         ],
@@ -614,6 +628,12 @@
         jnp.asarray(span),
         jnp.asarray(fwd),
     )
+    result = pl.pallas_call(
+        lay_out,
+        out_shape=jax.ShapeDtypeStruct((3, NPTS, LOCAL, ELEMS), F32),
+        in_specs=[vmem],
+        out_specs=vmem,
+    )(result)
     return jnp.transpose(result.reshape(3, NODES, NODES, LOCAL, ELEMS), (0, 3, 1, 2, 4))
 
 

time: 62.8 us -> 61.3 us (0.976)
  local copies, waits for them, and re-layouts: 1.85 us -> 0 us
    pallas_call x0 -> x1, Pallas kernels: none -> 2.54 us  [shards(): pl.pallas_call(lay_out, out_shape=jax.ShapeDtypeStruct((3, NPTS, LOCAL, E...]
    pallas_call x1, Pallas kernels: 60.8 us -> 58.6 us  [shards(): pl.pallas_call(functools.partial(kernel, n_dom), out_shape=jax.ShapeDtype...]
    unnamed x1 -> x0, local copies, waits for them, and re-layouts: 1.85 us -> none
where the time goes in v2:
time: 61.3 us; the launch traced here: 61.1 us
  Pallas kernels  61.1 us (100%)
    pallas_call x1, Pallas kernels, shards(): pl.pallas_call(functools.partial(kernel, n_dom), out_shape=jax.ShapeDtype...  58.6 us
    pallas_call x1, Pallas kernels, shards(): pl.pallas_call(lay_out, out_shape=jax.ShapeDtypeStruct((3, NPTS, LOCAL, E...  2.54 us

profile of v2, /device:TPU:1, one launch (start us, length us, event | category | flops | bytes accessed | tf_op | source)
XLA Modules:
  0.0 61.1 jit_solution(2797928906795381269)
XLA Ops:
  0.0 58.6 %shard_map.82.state = f32[3,96,128]{2,1,0:T(8,128)} custom-call(f32[3,81,4,32]{3,2,1,0:T(4,128)} %bitcast.10, f32[4,32]{1,0:T(4,128)} %met_ref.1, f32[12,2,10368]{2,1,0:T(2,128)} %bitcast.9, s32[5,1,24]{2,1,0:T(1,128)} %bitcast.11, s32[5,1,24]{2,1,0:T(1,128)} %bitcast.12, bf16[440,288]{1,0:T(8,128)(2,1)} %constant.6.clone.deriv_ref, ...), custom_call_target="tpu_custom_call" | custom-call | tf_op jit(solution)/shard_map/pallas_call | solution.py:577
  58.6 2.5 %shard_map.83 = f32[3,81,4,32]{3,2,1,0:T(4,128)} custom-call(f32[3,96,128]{2,1,0:T(8,128)} %shard_map.82.state), custom_call_target="tpu_custom_call" | custom-call | tf_op jit(solution)/shard_map/pallas_call | solution.py:631

commit v3 on v1

v3 whole, which is shorter than its diff:
```python
import functools

import jax
import jax.numpy as jnp
import ml_dtypes
import numpy as np
from jax import lax
from jax.experimental import pallas as pl
from jax.experimental.pallas import tpu as pltpu
from jax.sharding import PartitionSpec as P

MODES = 64
STEPS = 2
NODES = 9
NPTS = NODES * NODES
ELEMS = 32
PLANE = 16
LOCAL = MODES // PLANE
SPAN_PTS = NPTS * ELEMS // PLANE
CAP = 24
REACH = 2
STEP_SIZE = 0.01
VISCOSITY = 0.02

ROWS = 88
KROWS = 96
WIRE = 48
BACK = 8
REST = SPAN_PTS - 128
FLOWS = 12 * STEPS

F32 = jnp.float32
BF16 = jnp.bfloat16
MESH_ID = pl.DeviceIdType.MESH


def split_table(table):
    hi = table.astype(np.float32).astype(ml_dtypes.bfloat16)
    lo = (table - hi.astype(np.float64)).astype(np.float32).astype(ml_dtypes.bfloat16)
    return np.concatenate([hi, hi, lo], axis=1)


def derivative_tables():
    order = NODES - 1
    ids = np.arange(NODES)
    coords = -np.cos(np.pi * ids / order)
    weight = np.where((ids == 0) | (ids == order), 2.0, 1.0)
    table = np.zeros((NODES, NODES))
    for a in range(NODES):
        for i in range(NODES):
            if a != i:
                table[a, i] = weight[a] / weight[i] * (-1.0) ** (a + i) / (coords[a] - coords[i])
    table -= np.diag(table.sum(axis=1))
    eye = np.eye(NODES)
    along_xi, along_eta = np.kron(table, eye), np.kron(eye, table)
    ops = [
        along_xi,
        along_eta,
        along_xi @ along_xi,
        along_xi @ along_eta,
        along_eta @ along_eta,
    ]
    stacked = np.zeros((len(ops) * ROWS, KROWS))
    for at, op in enumerate(ops):
        stacked[at * ROWS : at * ROWS + NPTS, :NPTS] = op
    return split_table(stacked)


def span_tables():
    modes = np.arange(MODES)
    wave = (modes + 1) // 2
    cosine = (modes % 2 == 1) | (modes == 0)
    angles = 2.0 * np.pi * ((np.arange(MODES)[:, None] * wave[None, :]) % MODES) / MODES
    basis = np.where(cosine[None, :], np.cos(angles), np.sin(angles))
    slope = np.where(cosine[None, :], -wave * np.sin(angles), wave * np.cos(angles))
    scale = np.where((modes == 0) | (modes == MODES - 1), 1.0 / MODES, 2.0 / MODES)
    forward = basis.T * scale[:, None]
    order = (np.arange(PLANE)[None, :] * LOCAL + np.arange(LOCAL)[:, None]).reshape(-1)
    span = np.concatenate([basis[:, order], slope[:, order]], axis=0)
    return split_table(span), split_table(forward[order])


def halves(x):
    hi = x.astype(BF16)
    return hi, (x - hi.astype(F32)).astype(BF16)


def three(x):
    hi, lo = halves(x)
    return jnp.concatenate([hi, lo, hi], axis=0)


def dot(a, b):
    return jnp.dot(a, b, preferred_element_type=F32)


def swap_blocks(parts):
    shape = parts[0].shape
    lane = lax.broadcasted_iota(jnp.int32, shape, 1)
    even = (lane // 32) % 2 == 0
    low = lane < 64
    a0, a1, a2, a3 = parts

    def near(x, y):
        return (
            jnp.where(even, x, pltpu.roll(y, 32, 1)),
            jnp.where(even, pltpu.roll(x, 96, 1), y),
        )

    def far(x, y):
        moved = pltpu.roll(jnp.where(low, y, x), 64, 1)
        return jnp.where(low, x, moved), jnp.where(low, moved, y)

    b0, b1 = near(a0, a1)
    b2, b3 = near(a2, a3)
    c0, c2 = far(b0, b2)
    c1, c3 = far(b1, b3)
    return [c0, c1, c2, c3]


def turn(x, shift):
    return pltpu.roll(x, shift % 128, 1) if shift % 128 else x


STATE_AT = ((0, 8, 16), (0, 16, 32))
GRAD_AT = ((24, 32, 40), (8, 24, 40))
CHUNKS = (((0, 24), (24, 8), (32, 8), (40, 8)), ((0, 16), (16, 16), (32, 8), (40, 8)))
DISTANCES = (8, 7, 9, 6, 10, 5, 11, 4, 12, 3, 13, 2, 14, 1, 15)


def kernel(
    n_dom,
    adj_ref,
    met_ref,
    base_ref,
    edge_ref,
    flip_ref,
    deriv_ref,
    span_ref,
    fwd_ref,
    out_ref,
    state,
    grads,
    base_in,
    base_rows,
    base_head,
    base_tail,
    send_out,
    recv_out,
    send_back,
    recv_back,
    edge_out,
    edge_in,
    trace_a,
    trace_b,
    sums,
    send_hot,
    recv_hot,
    inv_weight,
    metrics,
    slot_ids,
    adj_in,
    met_in,
    deriv_in,
    edge_ids,
    flip_ids,
    span_in,
    fwd_in,
    load_sem,
    out_send,
    out_recv,
    back_send,
    back_recv,
    edge_send,
    edge_recv,
):
    dom = lax.axis_index("dom")
    me = lax.axis_index("plane")

    barrier = pltpu.get_barrier_semaphore()

    def greet(distance, carry):
        pl.semaphore_signal(
            barrier, inc=1, device_id=(dom, lax.rem(me + distance, PLANE)), device_id_type=MESH_ID
        )
        return carry

    lax.fori_loop(1, PLANE, greet, 0)
    others = [block for block in range(2 * REACH + 1) if block != REACH]
    for block in others:
        pl.semaphore_signal(
            barrier,
            inc=1,
            device_id=(lax.rem(dom + block - REACH + n_dom, n_dom), me),
            device_id_type=MESH_ID,
        )

    loads = {}
    for at, (name, source, target) in enumerate(
        (
            ("state", adj_ref, adj_in),
            ("metric", met_ref, met_in),
            ("deriv", deriv_ref, deriv_in),
            ("base", base_ref, base_in),
            ("edges", edge_ref, edge_ids),
            ("flips", flip_ref, flip_ids),
            ("span", span_ref, span_in),
            ("forward", fwd_ref, fwd_in),
        )
    ):
        loads[name] = pltpu.make_async_copy(source, target, load_sem.at[at])
        loads[name].start()

    def out_copy(step, chunk, distance):
        peer = lax.rem(me + distance, PLANE)
        start, rows = CHUNKS[step][chunk]
        return pltpu.make_async_remote_copy(
            src_ref=send_out.at[step, pl.ds(pl.multiple_of(peer * WIRE + start, 8), rows)],
            dst_ref=recv_out.at[step, pl.ds(pl.multiple_of(me * WIRE + start, 8), rows)],
            send_sem=out_send.at[step, chunk],
            recv_sem=out_recv.at[step, chunk],
            device_id=(dom, peer),
            device_id_type=MESH_ID,
        )

    def back_copy(step, comp, distance):
        peer = lax.rem(me + distance, PLANE)
        return pltpu.make_async_remote_copy(
            src_ref=send_back.at[step, comp, pl.ds(pl.multiple_of(peer * BACK, 8), BACK)],
            dst_ref=recv_back.at[step, comp, pl.ds(pl.multiple_of(me * BACK, 8), BACK)],
            send_sem=back_send.at[step, comp],
            recv_sem=back_recv.at[step, comp],
            device_id=(dom, peer),
            device_id_type=MESH_ID,
        )

    def edge_copy(step, comp, block):
        return pltpu.make_async_remote_copy(
            src_ref=edge_out.at[step, comp, pl.ds(block * CAP, CAP)],
            dst_ref=edge_in.at[step, comp, pl.ds((2 * REACH - block) * CAP, CAP)],
            send_sem=edge_send.at[step, comp],
            recv_sem=edge_recv.at[step, comp],
            device_id=(lax.rem(dom + block - REACH + n_dom, n_dom), me),
            device_id_type=MESH_ID,
        )

    def all_of(source, target, rows, send_sem, recv_sem):
        return pltpu.make_async_remote_copy(
            src_ref=source.at[pl.ds(0, rows)],
            dst_ref=target.at[pl.ds(0, rows)],
            send_sem=send_sem,
            recv_sem=recv_sem,
            device_id=(dom, lax.rem(me + 1, PLANE)),
            device_id_type=MESH_ID,
        )

    def all_out(step, chunk):
        rows = (PLANE - 1) * CHUNKS[step][chunk][1]
        sems = out_send.at[step, chunk], out_recv.at[step, chunk]
        return all_of(send_out.at[step], recv_out.at[step], rows, *sems)

    def all_back(step, comp):
        rows = (PLANE - 1) * BACK
        sems = back_send.at[step, comp], back_recv.at[step, comp]
        return all_of(send_back.at[step, comp], recv_back.at[step, comp], rows, *sems)

    def all_edges(step, comp):
        sems = edge_send.at[step, comp], edge_recv.at[step, comp]
        return all_of(edge_out.at[step, comp], edge_in.at[step, comp], 2 * REACH * CAP, *sems)

    def each_peer(what):
        for distance in DISTANCES:
            what(distance)

    loads["state"].wait()
    for comp in range(3):
        for mode in range(LOCAL):
            state[comp, 0:NPTS, ELEMS * mode : ELEMS * (mode + 1)] = adj_in[comp, :, mode, :]
        state[comp, NPTS:KROWS, :] = jnp.zeros((KROWS - NPTS, 128), F32)
    loads["metric"].wait()
    for row in range(4):
        for group in range(4):
            metrics[row : row + 1, ELEMS * group : ELEMS * (group + 1)] = met_in[row : row + 1, :]
    xi_x, xi_y = metrics[0:1, :], metrics[1:2, :]
    eta_x, eta_y = metrics[2:3, :], metrics[3:4, :]

    lane_row = lax.broadcasted_iota(jnp.int32, (1, 128), 1)
    owner_lane = lax.broadcasted_iota(jnp.int32, (PLANE, 128), 1)
    owner_start = 2 * lax.broadcasted_iota(jnp.int32, (PLANE, 128), 0)
    after = owner_lane >= owner_start
    places = []
    for comp in range(3):
        place = (owner_lane - owner_start + (128 - REST * comp)) % 128
        places.append(place < REST)
    wave = ((LOCAL * me + lane_row // ELEMS + 1) // 2).astype(F32)

    def split_state(comp):
        return three(state[comp])

    def derive(step, comp, rhs):
        first = dot(deriv_in[0 : 2 * ROWS, :], rhs)
        along_xi, along_eta = first[0:ROWS, :], first[ROWS : 2 * ROWS, :]
        grads[2 * comp, 0:ROWS, :] = xi_x * along_xi + eta_x * along_eta
        grads[2 * comp + 1, 0:ROWS, :] = xi_y * along_xi + eta_y * along_eta

        def nodes(field, k):
            rows = pl.ds(k, PLANE, stride=5)
            return grads[2 * comp + field - 1, rows, :] if field else state[comp, rows, :]

        zeros = jnp.zeros((PLANE, 128), F32)

        def put(at, mode, rows):
            send_out[step, pl.ds(at + mode, PLANE, stride=WIRE), :] = rows

        early = swap_blocks([nodes(0, 4), nodes(0, 5), nodes(1, 4), nodes(1, 5)])
        late = swap_blocks([nodes(2, 4), nodes(2, 5), zeros, zeros])
        packed = [zeros] * LOCAL
        to = (STATE_AT[step][comp], GRAD_AT[step][comp], GRAD_AT[step][comp] + LOCAL)
        for field in range(3):
            heads = swap_blocks([nodes(field, k) for k in range(4)])
            both, side = (late, 0) if field == 2 else (early, 64 * field)
            for mode in range(LOCAL):
                put(to[field], mode, jnp.where(after, heads[mode], turn(both[mode], -side)))
                packed[mode] = jnp.where(
                    places[field], turn(both[mode], REST * field - side), packed[mode]
                )
        for mode in range(LOCAL):
            put(STATE_AT[step][comp] + LOCAL, mode, packed[mode])

    def send_chunk(step, chunk):
        each_peer(lambda distance: out_copy(step, chunk, distance).start())

    def keep_chunk(step, chunk):
        start, rows = CHUNKS[step][chunk]
        mine = pl.ds(pl.multiple_of(me * WIRE + start, 8), rows)
        recv_out[step, mine, :] = send_out[step, mine, :]

    def diffuse(comp, rhs):
        second = dot(deriv_in[2 * ROWS : 5 * ROWS, :], rhs)
        factor = STEP_SIZE * VISCOSITY
        keep = 1.0 - factor * (wave * wave)
        both_xi = factor * (xi_x * xi_x + xi_y * xi_y)
        mixed = (2.0 * factor) * (xi_x * eta_x + xi_y * eta_y)
        both_eta = factor * (eta_x * eta_x + eta_y * eta_y)
        state[comp, 0:ROWS, :] = keep * state[comp, 0:ROWS, :] + (
            both_xi * second[0:ROWS, :]
            + mixed * second[ROWS : 2 * ROWS, :]
            + both_eta * second[2 * ROWS : 3 * ROWS, :]
        )

    def gather_base():
        loads["base"].wait()

        def gather(block, carry):
            lanes = pl.ds(pl.multiple_of(128 * block, 128), 128)
            rows = pl.ds(pl.multiple_of(FLOWS * block, 8), FLOWS)
            base_rows[rows, :] = base_in[:, :, lanes].reshape(FLOWS, 128)
            return carry

        lax.fori_loop(0, NPTS, gather, 0)
        base_rows[FLOWS * NPTS :, :] = jnp.zeros((2 * FLOWS, 128), F32)

    def arrange_base():
        lane = lax.broadcasted_iota(jnp.int32, (FLOWS, 128), 1)
        point = (lane - 2 * me + 128) % 128

        def body(n, carry):
            start = SPAN_PTS * n
            block = start // 128
            shift = start - 128 * block
            back = lax.rem(128 - shift + 2 * me, 128)
            early = point < 128 - shift
            rolled = []
            for at in range(3):
                rows = pl.ds(pl.multiple_of(FLOWS * (block + at), 8), FLOWS)
                rolled.append(pltpu.roll(base_rows[rows, :], back, 1))
            to = pl.ds(n, FLOWS, stride=MODES)
            base_head[to, :] = jnp.where(early, rolled[0], rolled[1])
            base_tail[to, :] = jnp.where(
                point < REST, jnp.where(early, rolled[1], rolled[2]), 0.0
            )
            return carry

        lax.fori_loop(0, MODES, body, 0)

    def prepare_edges():
        loads["edges"].wait()
        loads["flips"].wait()
        slot_ids[...] = jnp.full((16, 128), -1, jnp.int32)
        for block in range(2 * REACH + 1):
            lanes = slice(CAP * block, CAP * (block + 1))
            slot_ids[0:1, lanes] = edge_ids[block]
            slot_ids[8:9, lanes] = flip_ids[block]
        own, flip = slot_ids[0:1, :], slot_ids[8:9, :]
        odd = lane_row % 2 == 1
        paired = jnp.where(odd, pltpu.roll(own, 1, 1), pltpu.roll(own, 127, 1))
        inner = (lane_row >= CAP * REACH) & (lane_row < CAP * (REACH + 1))
        given = jnp.where(inner, paired, own)
        edge_row = lax.broadcasted_iota(jnp.int32, (128, 128), 0)
        hot = jnp.where(edge_row == own, 1.0, 0.0).astype(F32)
        recv_hot[:, 0:128] = hot.astype(BF16)
        recv_hot[:, 128:256] = hot.astype(BF16)
        gave = jnp.where(edge_row == given, 1.0, 0.0).astype(F32)
        turned = jnp.where(flip == 1, gave, 0.0)
        straight = (gave - turned).T.astype(BF16)
        turned = turned.T.astype(BF16)
        for part in range(2):
            send_hot[:, 256 * part : 256 * part + 128] = straight
            send_hot[:, 256 * part + 128 : 256 * part + 256] = turned
        counts = jnp.sum(hot.T, axis=0, keepdims=True)
        spread = []
        for edge in range(4):
            one = jnp.where(lane_row // ELEMS == edge, counts, 0.0)
            one = one + pltpu.roll(one, 64, 1)
            spread.append(one + pltpu.roll(one, 32, 1))
        inv_weight[...] = jnp.ones((KROWS, 128), F32)
        for edge, rows in enumerate(edge_rows):
            inv_weight[rows, :] = inv_weight[rows, :] + spread[edge]
        inv_weight[...] = 1.0 / inv_weight[...]
        trace_b[...] = jnp.zeros((128, 256), F32)

    def physical(step):
        def column(at):
            return jnp.concatenate(
                [
                    recv_out[step, pl.ds(at + mode, PLANE, stride=WIRE), :]
                    for mode in range(LOCAL)
                ],
                axis=0,
            )

        for chunk in range(1 if step == 0 else 3):
            all_out(step, chunk).wait_recv()
        columns = []
        for comp in range(3):
            columns += [column(STATE_AT[step][comp]), column(STATE_AT[step][comp] + LOCAL)]
        of_state = dot(span_in[...], three(jnp.concatenate(columns, axis=1)))

        def flow(base, index):
            row = MODES * (STEPS * index + step)
            return base[row : row + MODES, :]

        def product(comp, base, side, along_x, along_y):
            def now(i, slope=False):
                lanes = 128 * (2 * i + side)
                rows = slice(MODES, 2 * MODES) if slope else slice(0, MODES)
                return of_state[rows, lanes : lanes + 128]

            term = (
                flow(base, 0) * along_x + flow(base, 1) * along_y + flow(base, 2) * now(comp, True)
            )
            return term - (
                now(0) * flow(base, 3 + comp)
                + now(1) * flow(base, 6 + comp)
                + now(2) * flow(base, 9 + comp)
            )

        for comp in range(3):
            if step == 0 or comp == 2:
                all_out(step, comp + 1).wait_recv()
            at = GRAD_AT[step][comp]
            rhs = three(jnp.concatenate([column(at), column(at + LOCAL)], axis=1))
            of_grads = dot(span_in[0:MODES, :], rhs)
            first = product(comp, base_head, 0, of_grads[:, 0:128], of_grads[:, 128:256])
            rest_now = of_state[0:MODES, 128 * (2 * comp + 1) : 128 * (2 * comp + 2)]
            rest = product(comp, base_tail, 1, turn(rest_now, -REST), turn(rest_now, -2 * REST))
            back = dot(fwd_in[...], three(jnp.concatenate([first, rest], axis=1)))
            for at in range(2):
                for mode in range(LOCAL):
                    send_back[step, comp, pl.ds(at * LOCAL + mode, PLANE, stride=BACK), :] = back[
                        PLANE * mode : PLANE * (mode + 1), 128 * at : 128 * at + 128
                    ]
            each_peer(lambda distance, comp=comp: back_copy(step, comp, distance).start())
            mine = pl.ds(pl.multiple_of(me * BACK, 8), BACK)
            recv_back[step, comp, mine, :] = send_back[step, comp, mine, :]

    first_col, last_col = pl.ds(0, NODES, stride=NODES), pl.ds(8, NODES, stride=NODES)
    edge_rows = (first_col, slice(72, 81), last_col, slice(0, 9))

    def update(step, comp):
        all_back(step, comp).wait_recv()

        def came(at):
            return recv_back[step, comp, pl.ds(at, PLANE, stride=BACK), :]

        firsts, lasts = [], []
        for mode in range(LOCAL):
            moved = came(mode)
            last = jnp.where(places[0], came(LOCAL + mode), 0.0)
            firsts.append(jnp.where(after, moved, 0.0))
            lasts.append(jnp.where(after, last, moved))
        for k, rate in enumerate(swap_blocks(firsts) + swap_blocks(lasts)[:2]):
            rows = pl.ds(k, PLANE, stride=5)
            state[comp, rows, :] = state[comp, rows, :] + STEP_SIZE * rate

    def give_edges(step, comp):
        traces = swap_blocks([state[comp, rows, :] for rows in edge_rows])
        for mode in range(LOCAL):
            trace_a[mode * 16 : mode * 16 + NODES, :] = traces[mode]
        for i in range(NODES):
            rows = trace_a[pl.ds(i, LOCAL, stride=16), :]
            trace_b[LOCAL * i : LOCAL * (i + 1), 0:128] = rows
            trace_b[LOCAL * (8 - i) : LOCAL * (9 - i), 128:256] = rows
        hi, lo = halves(trace_b[...])
        given = lax.dot_general(
            send_hot[...],
            jnp.concatenate([hi, lo], axis=1),
            (((1,), (1,)), ((), ())),
            preferred_element_type=F32,
        )
        edge_out[step, comp] = given
        for block in others:
            edge_copy(step, comp, block).start()
        inner = slice(CAP * REACH, CAP * (REACH + 1))
        edge_in[step, comp, inner, :] = given[inner, :]
        edge_in[step, comp, 120:128, :] = jnp.zeros((8, 128), F32)

    def take_edges(step, comp):
        all_edges(step, comp).wait_recv()
        hi, lo = halves(edge_in[step, comp])
        sums[...] = dot(recv_hot[...], jnp.concatenate([hi, lo], axis=0)).T
        parts = swap_blocks([sums[pl.ds(mode, NODES, stride=LOCAL), :] for mode in range(LOCAL)])
        for rows, part in zip(edge_rows, parts):
            state[comp, rows, :] = state[comp, rows, :] + part
        state[comp, 0:ROWS, :] = state[comp, 0:ROWS, :] * inv_weight[0:ROWS, :]

    loads["deriv"].wait()
    halved = [split_state(comp) for comp in range(3)]
    for comp in range(3):
        derive(0, comp, halved[comp])
    prepare_edges()
    gather_base()
    pl.semaphore_wait(barrier, PLANE - 1 + len(others))
    for chunk in range(4):
        send_chunk(0, chunk)
    for chunk in range(4):
        keep_chunk(0, chunk)
    for comp in range(3):
        diffuse(comp, halved[comp])
    arrange_base()
    loads["span"].wait()
    loads["forward"].wait()
    physical(0)
    for comp in range(3):
        update(0, comp)
        give_edges(0, comp)
    halved = []
    for comp in range(3):
        take_edges(0, comp)
        halved.append(split_state(comp))
        derive(1, comp, halved[comp])
        for chunk in (comp,) if comp < 2 else (2, 3):
            send_chunk(1, chunk)
    for chunk in range(4):
        keep_chunk(1, chunk)
    for comp in range(3):
        diffuse(comp, halved[comp])
    physical(1)
    for comp in range(3):
        update(1, comp)
        give_edges(1, comp)
    for comp in range(3):
        take_edges(1, comp)
        out_ref[comp] = state[comp, 0:NPTS, :]

    for step in range(STEPS):
        for chunk in range(4):
            all_out(step, chunk).wait_send()
        for comp in range(3):
            all_back(step, comp).wait_send()
            all_edges(step, comp).wait_send()


def shards(n_dom, adjoint, metric, base_flow, edge_list, flips):
    state_in = jnp.transpose(adjoint, (0, 2, 3, 1, 4)).reshape(3, NPTS, LOCAL, ELEMS)
    base_in = jnp.transpose(base_flow, (1, 0, 2))
    deriv = derivative_tables()
    span, fwd = span_tables()
    vmem = pl.BlockSpec(memory_space=pltpu.VMEM)
    dma = pltpu.SemaphoreType.DMA
    result = pl.pallas_call(
        functools.partial(kernel, n_dom),
        out_shape=jax.ShapeDtypeStruct((3, NPTS, 128), F32),
        in_specs=[pl.BlockSpec(memory_space=pltpu.HBM)] * 8,
        out_specs=vmem,
        scratch_shapes=[
            pltpu.VMEM((3, KROWS, 128), F32),
            pltpu.VMEM((6, KROWS, 128), F32),
            pltpu.VMEM((12, STEPS, 128 * NPTS), F32),
            pltpu.VMEM((FLOWS * (NPTS + 2), 128), F32),
            pltpu.VMEM((FLOWS * MODES, 128), F32),
            pltpu.VMEM((FLOWS * MODES, 128), F32),
            pltpu.VMEM((STEPS, PLANE * WIRE, 128), F32),
            pltpu.VMEM((STEPS, PLANE * WIRE, 128), F32),
            pltpu.VMEM((STEPS, 3, PLANE * BACK, 128), F32),
            pltpu.VMEM((STEPS, 3, PLANE * BACK, 128), F32),
            pltpu.VMEM((STEPS, 3, 128, 128), F32),
            pltpu.VMEM((STEPS, 3, 128, 128), F32),
            pltpu.VMEM((LOCAL * 16, 128), F32),
            pltpu.VMEM((128, 256), F32),
            pltpu.VMEM((128, 128), F32),
            pltpu.VMEM((128, 512), BF16),
            pltpu.VMEM((128, 256), BF16),
            pltpu.VMEM((KROWS, 128), F32),
            pltpu.VMEM((8, 128), F32),
            pltpu.VMEM((16, 128), jnp.int32),
            pltpu.VMEM((3, NPTS, LOCAL, ELEMS), F32),
            pltpu.VMEM((4, ELEMS), F32),
            pltpu.VMEM(deriv.shape, BF16),
            pltpu.VMEM((2 * REACH + 1, 1, CAP), jnp.int32),
            pltpu.VMEM((2 * REACH + 1, 1, CAP), jnp.int32),
            pltpu.VMEM(span.shape, BF16),
            pltpu.VMEM(fwd.shape, BF16),
            dma((8,)),
            dma((STEPS, 4)),
            dma((STEPS, 4)),
            dma((STEPS, 3)),
            dma((STEPS, 3)),
            dma((STEPS, 3)),
            dma((STEPS, 3)),
        ],
        compiler_params=pltpu.CompilerParams(
            collective_id=0, has_side_effects=True, vmem_limit_bytes=58 * 1024 * 1024
        ),
    )(
        state_in,
        metric,
        base_in,
        jnp.transpose(edge_list, (1, 0, 2)),
        jnp.transpose(flips, (1, 0, 2)),
        jnp.asarray(deriv),
        jnp.asarray(span),
        jnp.asarray(fwd),
    )
    return jnp.transpose(result.reshape(3, NODES, NODES, LOCAL, ELEMS), (0, 3, 1, 2, 4))


def solution(mesh):
    placed = (
        P(None, "plane", None, None, "dom"),
        P(None, "dom"),
        P(None, None, ("dom", "plane")),
        P("dom", None, None),
        P("dom", None, None),
    )
    return jax.shard_map(
        functools.partial(shards, mesh.shape["dom"]),
        mesh=mesh,
        in_specs=placed,
        out_specs=P(None, "plane", None, None, "dom"),
        check_vma=False,
    )
```

time: 62.8 us -> 60.2 us (0.959)
  Pallas kernels: 60.8 us -> 58.1 us
    pallas_call x1, Pallas kernels: 60.8 us -> 58.1 us  [shards(): pl.pallas_call(functools.partial(kernel, n_dom), out_shape=jax.ShapeDtype...]
    reshape x0 -> x1, local copies, waits for them, and re-layouts: none -> 1.94 us  [shards(): result.reshape(3, NODES, NODES, LOCAL, ELEMS)]
    unnamed x1 -> x0, local copies, waits for them, and re-layouts: 1.85 us -> none
where the time goes in v3:
time: 60.2 us; the launch traced here: 60 us
  Pallas kernels  58.1 us (97%)
  local copies, waits for them, and re-layouts  1.94 us (3%)
    pallas_call x1, Pallas kernels, shards(): pl.pallas_call(functools.partial(kernel, n_dom), out_shape=jax.ShapeDtype...  58.1 us
    reshape x1, local copies, waits for them, and re-layouts, shards(): result.reshape(3, NODES, NODES, LOCAL, ELEMS)  1.94 us

profile of v3, /device:TPU:1, one launch (start us, length us, event | category | flops | bytes accessed | tf_op | source)
XLA Modules:
  0.0 60.0 jit_solution(1252013922406726047)
XLA Ops:
  0.0 58.1 %shard_map.82 = f32[3,81,128]{2,1,0:T(8,128)} custom-call(f32[3,81,4,32]{3,2,1,0:T(4,128)} %bitcast.8, f32[4,32]{1,0:T(4,128)} %met_ref.1, f32[12,2,10368]{2,1,0:T(2,128)} %bitcast.7, s32[5,1,24]{2,1,0:T(1,128)} %bitcast.9, s32[5,1,24]{2,1,0:T(1,128)} %bitcast.10, bf16[440,288]{1,0:T(8,128)(2,1)} %constant.6.clone.deriv_ref, ...), custom_call_target="tpu_custom_call" | custom-call | tf_op jit(solution)/shard_map/pallas_call | solution.py:581
  58.1 1.9 %reshape.7 = f32[3,9,9,4,32]{4,3,2,1,0:T(4,128)} reshape(f32[3,81,128]{2,1,0:T(8,128)} %shard_map.82) | data formatting | bytes 248832 | tf_op jit(solution)/shard_map/reshape | solution.py:635

commit v4 on v3

--- a/solution.py
+++ b/solution.py
@@ -125,7 +125,7 @@
 STATE_AT = ((0, 8, 16), (0, 16, 32))
 GRAD_AT = ((24, 32, 40), (8, 24, 40))
 CHUNKS = (((0, 24), (24, 8), (32, 8), (40, 8)), ((0, 16), (16, 16), (32, 8), (40, 8)))
-DISTANCES = (8, 7, 9, 6, 10, 5, 11, 4, 12, 3, 13, 2, 14, 1, 15)
+DISTANCES = (8, 9, 7, 6, 10, 11, 5, 4, 12, 13, 3, 2, 14, 15, 1)
 
 
 def kernel(
@@ -167,6 +167,7 @@
     span_in,
     fwd_in,
     load_sem,
+    store_sem,
     out_send,
     out_recv,
     back_send,
@@ -179,14 +180,11 @@
 
     barrier = pltpu.get_barrier_semaphore()
 
-    def greet(distance, carry):
+    others = [0, 4, 1, 3]
+    for distance in DISTANCES:
         pl.semaphore_signal(
             barrier, inc=1, device_id=(dom, lax.rem(me + distance, PLANE)), device_id_type=MESH_ID
         )
-        return carry
-
-    lax.fori_loop(1, PLANE, greet, 0)
-    others = [block for block in range(2 * REACH + 1) if block != REACH]
     for block in others:
         pl.semaphore_signal(
             barrier,
@@ -417,7 +415,9 @@
         for edge, rows in enumerate(edge_rows):
             inv_weight[rows, :] = inv_weight[rows, :] + spread[edge]
         inv_weight[...] = 1.0 / inv_weight[...]
-        trace_b[...] = jnp.zeros((128, 256), F32)
+        trace_b[...] = jnp.zeros((40, 256), F32)
+        edge_out[...] = jnp.zeros((STEPS, 3, 128, 128), F32)
+        edge_in[:, :, 120:128, :] = jnp.zeros((STEPS, 3, 8, 128), F32)
 
     def physical(step):
         def column(at):
@@ -508,12 +508,11 @@
             (((1,), (1,)), ((), ())),
             preferred_element_type=F32,
         )
-        edge_out[step, comp] = given
+        edge_out[step, comp, :, 0:40] = given
         for block in others:
             edge_copy(step, comp, block).start()
         inner = slice(CAP * REACH, CAP * (REACH + 1))
-        edge_in[step, comp, inner, :] = given[inner, :]
-        edge_in[step, comp, 120:128, :] = jnp.zeros((8, 128), F32)
+        edge_in[step, comp, inner, :] = edge_out[step, comp, inner, :]
 
     def take_edges(step, comp):
         all_edges(step, comp).wait_recv()
@@ -559,16 +558,22 @@
     for comp in range(3):
         update(1, comp)
         give_edges(1, comp)
-    for comp in range(3):
-        take_edges(1, comp)
-        out_ref[comp] = state[comp, 0:NPTS, :]
-
     for step in range(STEPS):
         for chunk in range(4):
             all_out(step, chunk).wait_send()
         for comp in range(3):
             all_back(step, comp).wait_send()
             all_edges(step, comp).wait_send()
+    stores = []
+    for comp in range(3):
+        take_edges(1, comp)
+        store = pltpu.make_async_copy(
+            state.at[comp, pl.ds(0, NPTS)], out_ref.at[comp], store_sem.at[comp]
+        )
+        store.start()
+        stores.append(store)
+    for store in stores:
+        store.wait()
 
 
 def shards(n_dom, adjoint, metric, base_flow, edge_list, flips):
@@ -576,13 +581,12 @@
     base_in = jnp.transpose(base_flow, (1, 0, 2))
     deriv = derivative_tables()
     span, fwd = span_tables()
-    vmem = pl.BlockSpec(memory_space=pltpu.VMEM)
     dma = pltpu.SemaphoreType.DMA
     result = pl.pallas_call(
         functools.partial(kernel, n_dom),
         out_shape=jax.ShapeDtypeStruct((3, NPTS, 128), F32),
         in_specs=[pl.BlockSpec(memory_space=pltpu.HBM)] * 8,
-        out_specs=vmem,
+        out_specs=pl.BlockSpec(memory_space=pltpu.HBM),
         scratch_shapes=[
             pltpu.VMEM((3, KROWS, 128), F32),
             pltpu.VMEM((6, KROWS, 128), F32),
@@ -597,7 +601,7 @@
             pltpu.VMEM((STEPS, 3, 128, 128), F32),
             pltpu.VMEM((STEPS, 3, 128, 128), F32),
             pltpu.VMEM((LOCAL * 16, 128), F32),
-            pltpu.VMEM((128, 256), F32),
+            pltpu.VMEM((40, 256), F32),
             pltpu.VMEM((128, 128), F32),
             pltpu.VMEM((128, 512), BF16),
             pltpu.VMEM((128, 256), BF16),
@@ -612,6 +616,7 @@
             pltpu.VMEM(span.shape, BF16),
             pltpu.VMEM(fwd.shape, BF16),
             dma((8,)),
+            dma((3,)),
             dma((STEPS, 4)),
             dma((STEPS, 4)),
             dma((STEPS, 3)),

time: 60.2 us -> 60 us (level)
  no operation moved by 1% of the time
where the time goes in v4:
time: 60 us; the launch traced here: 59.8 us
  Pallas kernels  57.9 us (96%)
  local copies, waits for them, and re-layouts  1.94 us (3%)
    pallas_call x1, Pallas kernels, shards(): pl.pallas_call(functools.partial(kernel, n_dom), out_shape=jax.ShapeDtype...  57.9 us
    reshape x1, local copies, waits for them, and re-layouts, shards(): result.reshape(3, NODES, NODES, LOCAL, ELEMS)  1.94 us

profile of v4, /device:TPU:1, one launch (start us, length us, event | category | flops | bytes accessed | tf_op | source)
XLA Modules:
  0.0 59.8 jit_solution(17590215971676023459)
XLA Ops:
  0.0 57.9 %shard_map.82 = f32[3,81,128]{2,1,0:T(8,128)} custom-call(f32[3,81,4,32]{3,2,1,0:T(4,128)} %bitcast.8, f32[4,32]{1,0:T(4,128)} %met_ref.1, f32[12,2,10368]{2,1,0:T(2,128)} %bitcast.7, s32[5,1,24]{2,1,0:T(1,128)} %bitcast.9, s32[5,1,24]{2,1,0:T(1,128)} %bitcast.10, bf16[440,288]{1,0:T(8,128)(2,1)} %constant.6.clone.deriv_ref, ...), custom_call_target="tpu_custom_call" | custom-call | tf_op jit(solution)/shard_map/pallas_call | solution.py:585
  57.9 1.9 %reshape.7 = f32[3,9,9,4,32]{4,3,2,1,0:T(4,128)} reshape(f32[3,81,128]{2,1,0:T(8,128)} %shard_map.82) | data formatting | bytes 248832 | tf_op jit(solution)/shard_map/reshape | solution.py:640

commit v5 on v4

--- a/solution.py
+++ b/solution.py
@@ -527,7 +527,6 @@
     halved = [split_state(comp) for comp in range(3)]
     for comp in range(3):
         derive(0, comp, halved[comp])
-    prepare_edges()
     gather_base()
     pl.semaphore_wait(barrier, PLANE - 1 + len(others))
     for chunk in range(4):
@@ -537,6 +536,7 @@
     for comp in range(3):
         diffuse(comp, halved[comp])
     arrange_base()
+    prepare_edges()
     loads["span"].wait()
     loads["forward"].wait()
     physical(0)

time: 60 us -> 60.3 us (level)
  no operation moved by 1% of the time
where the time goes in v5:
time: 60.3 us; the launch traced here: 60.1 us
  Pallas kernels  58.2 us (97%)
  local copies, waits for them, and re-layouts  1.94 us (3%)
    pallas_call x1, Pallas kernels, shards(): pl.pallas_call(functools.partial(kernel, n_dom), out_shape=jax.ShapeDtype...  58.2 us
    reshape x1, local copies, waits for them, and re-layouts, shards(): result.reshape(3, NODES, NODES, LOCAL, ELEMS)  1.94 us

profile of v5, /device:TPU:1, one launch (start us, length us, event | category | flops | bytes accessed | tf_op | source)
XLA Modules:
  0.0 60.1 jit_solution(10484183256480599693)
XLA Ops:
  0.0 58.2 %shard_map.82 = f32[3,81,128]{2,1,0:T(8,128)} custom-call(f32[3,81,4,32]{3,2,1,0:T(4,128)} %bitcast.8, f32[4,32]{1,0:T(4,128)} %met_ref.1, f32[12,2,10368]{2,1,0:T(2,128)} %bitcast.7, s32[5,1,24]{2,1,0:T(1,128)} %bitcast.9, s32[5,1,24]{2,1,0:T(1,128)} %bitcast.10, bf16[440,288]{1,0:T(8,128)(2,1)} %constant.6.clone.deriv_ref, ...), custom_call_target="tpu_custom_call" | custom-call | tf_op jit(solution)/shard_map/pallas_call | solution.py:585
  58.2 1.9 %reshape.7 = f32[3,9,9,4,32]{4,3,2,1,0:T(4,128)} reshape(f32[3,81,128]{2,1,0:T(8,128)} %shard_map.82) | data formatting | bytes 248832 | tf_op jit(solution)/shard_map/reshape | solution.py:640
